TPU v7x, 256 devices: a whole 4x4x8 slice. The times are simulated.
256 devices in a mesh: img: 32 (over z, y_hi, core), ori: 8 (over x, y_lo).
Axes of the slice: x: 4, y: 4 (y_hi: 2, y_lo: 2; y = y_hi * 2 + y_lo), z: 8, core: 2. Of those that a mesh axis runs over, the one named last changes fastest.
Arguments:
- images: float32 [32768, 2048], P(('img', 'ori')), may hold values from -40 to 40
- precision: float32 [32768], P('img'), may hold values from 0.5 to 2
- projections: bfloat16 [8192, 2048], P('ori'), may hold values from -1 to 1
- tile_mask: int32 [256, 64], P('img', 'ori'), may hold values from 0 to 1, as said below
Outputs:
- posteriors: bfloat16 [32768, 8192], P('img', 'ori')
- references: float32 [8192, 2048], P(('ori', 'img'))
Inputs may be any that keep to these rules, and one draw needn't show every extreme that they name: `tile_mask`: every image block has at least one live tile.
All inputs are finite; a program needn't handle non-finite values.
Results may differ from a plain program's by a relative error of at most 0.0095.
Values may be sent and summed in bfloat16 or wider, within the bound.
A program may use at most 64 MiB of HBM per device.

v0:
```python
import jax
import jax.numpy as jnp
from jax import lax
from jax.sharding import PartitionSpec as P

prior_weight = 1.0
very_low = -1e30


def weighted_sums(weights, rows_block):
    return lax.dot_general(
        weights, rows_block, (((0,), (0,)), ((), ())), preferred_element_type=jnp.float32
    )


def body(images, precision, projections, tile_mask):
    lowered = images.astype(jnp.bfloat16)
    grouped = lax.all_gather(lowered, "ori", axis=0, tiled=True)
    proj_float = projections.astype(jnp.float32)
    squared = jnp.sum(proj_float * proj_float, axis=1)
    blocks, tiles_here = tile_mask.shape
    per_block = grouped.shape[0] // blocks
    tile_width = projections.shape[0] // tiles_here
    products = lax.dot_general(
        grouped, projections, (((1,), (1,)), ((), ())), preferred_element_type=jnp.float32
    )
    scores = precision[:, None] * (products - 0.5 * squared[None, :])
    shaped = scores.reshape(blocks, per_block, tiles_here, tile_width)
    alive = jnp.broadcast_to((tile_mask > 0)[:, None, :, None], shaped.shape)
    masked = jnp.where(alive, shaped, very_low)
    local_high = jnp.max(masked, axis=(2, 3))
    row_high = lax.pmax(local_high, "ori")
    local_total = jnp.sum(
        jnp.where(alive, jnp.exp(masked - row_high[:, :, None, None]), 0.0), axis=(2, 3)
    )
    row_total = lax.psum(local_total, "ori")
    probable = (
        jnp.where(alive, jnp.exp(masked - row_high[:, :, None, None]), 0.0)
        / row_total[:, :, None, None]
    )
    posteriors = probable.reshape(scores.shape).astype(jnp.bfloat16)
    counts = jnp.sum(posteriors.astype(jnp.float32), axis=0)
    summed, totals = (
        lax.psum_scatter(
            weighted_sums(posteriors, grouped), "img", scatter_dimension=0, tiled=True
        ),
        lax.psum_scatter(counts, "img", scatter_dimension=0, tiled=True),
    )
    rows_here = summed.shape[0]
    first_row = lax.axis_index("img") * rows_here
    prior_rows = lax.dynamic_slice_in_dim(proj_float, first_row, rows_here, 0)
    refined = (summed + prior_weight * prior_rows) / (totals[:, None] + prior_weight)
    return (posteriors, refined)


def solution(mesh):
    return jax.shard_map(
        body,
        mesh=mesh,
        in_specs=(P(("img", "ori"), None), P("img"), P("ori", None), P("img", "ori")),
        out_specs=(P("img", "ori"), P(("ori", "img"), None)),
        check_vma=False,
    )
```

profile of v0, /device:TPU:2, one launch (start us, length us, event | category | flops | bytes accessed | tf_op | source)
XLA Modules:
  0.0 328.1 jit_solution(5797426212921994888)
XLA Ops:
  7.2 0.0 all-gather.2.cloned.1.call-start
  7.2 2.1 convert_element_type.12
  9.3 0.0 all-gather.2.cloned.1.call-update
  9.3 0.0 reduce-scatter.2.cloned.1.call-start
  9.4 0.7 broadcast_compare_fusion
  10.1 0.1 copy.8
  10.2 3.1 multiply_reduce_fusion
  13.2 92.3 %all-gather.2.cloned.1.call-done = bf16[1024,2048]{1,0:T(8,128)(2,1)} async-done(((bf16[128,2048]{1,0:T(8,128)(2,1)}), bf16[1024,2048]{1,0:T(8,128)(2,1)}) %all-gather.2.cloned.1.call-update) | async-done | bytes 4194320 | tf_op jit(solution)/shard_map/all_gather | solution.py:18
  105.5 0.3 broadcast_in_dim.22
  105.9 10.2 %fusion = (f32[1024]{0:T(1024)S(1)}, f32[1024,1024]{0,1:T(8,128)}) fusion(pred[128,8,8,128]{3,2,1,0:T(8,128)(4,1)S(1)} %bitcast.21, f32[1024]{0:T(1024)S(1)} %broadcast_multiply_fusion, f32[1024]{0:T(1024)S(1)} %copy-done, bf16[1024,2048]{1,0:T(8,128)(2,1)} %all-gather.2.cloned.1.call-done, bf16[1024,2048]{1,0:T(8,128)(2,1)} %param.6), kind=kOutput, calls=%fused_computation.5 | convolution fusion | flops 4299160576 | bytes 13643776 | tf_op jit(solution)/shard_map/dot_general | solution.py:24
  116.1 16.3 %pmax.7 = f32[1024]{0:T(1024)S(1)} all-reduce(f32[1024]{0:T(1024)S(1)} %get-tuple-element.8), channel_id=1, replica_groups=mesh['img'=32,'ori'=8] {'ori'}, use_global_device_ids=true, to_apply=%region_2.3 | all-reduce | flops 1024 | bytes 8192 | tf_op jit(solution)/shard_map/pmax | solution.py:32
  132.4 3.7 %fusion.1 = f32[1024]{0:T(1024)S(1)} fusion(f32[1024]{0:T(1024)S(1)} %pmax.7, f32[1024,1024]{0,1:T(8,128)} %get-tuple-element.9, f32[1024]{0:T(1024)S(1)} %broadcast_multiply_fusion, f32[1024]{0:T(1024)S(1)} %copy-done, pred[128,8,8,128]{3,2,1,0:T(8,128)(4,1)S(1)} %bitcast.22), kind=kLoop, calls=%fused_computation.6 | loop fusion | flops 6290432 | bytes 5259264 | tf_op jit(solution)/shard_map/reduce_sum | solution.py:33
  136.1 16.0 %psum.7 = f32[1024]{0:T(1024)S(1)} all-reduce(f32[1024]{0:T(1024)S(1)} %fusion.1), channel_id=1, replica_groups=mesh['img'=32,'ori'=8] {'ori'}, use_global_device_ids=true, to_apply=%region_4.5 | all-reduce | flops 1024 | bytes 8192 | tf_op jit(solution)/shard_map/psum | solution.py:36
  152.0 4.0 %convert_reduce_fusion = (f32[1024]{0:T(1024)S(1)}, bf16[1024,1024]{0,1:T(8,128)(2,1)S(1)}) fusion(f32[1024]{0:T(1024)S(1)} %psum.7, f32[1024]{0:T(1024)S(1)} %pmax.7, f32[1024,1024]{0,1:T(8,128)} %get-tuple-element.9, f32[1024]{0:T(1024)S(1)} %broadcast_multiply_fusion, f32[1024]{0:T(1024)S(1)} %copy-done, pred[128,8,8,128]{3,2,1,0:T(8,128)(4,1)S(1)} %bitcast.23), kind=kLoop, calls=%fused_computation.1 | loop fusion | flops 9436160 | bytes 7360512 | tf_op jit(solution)/shard_map/reduce_sum | solution.py:42
  156.0 6.6 %fusion.2 = f32[1024,2048]{1,0:T(8,128)} fusion(bf16[1024,1024]{0,1:T(8,128)(2,1)S(1)} %get-tuple-element.7, bf16[1024,2048]{1,0:T(8,128)(2,1)S(1)} %copy-done.1), kind=kOutput, calls=%fused_computation.11 | convolution fusion | flops 4294967296 | bytes 14680064 | tf_op jit(solution)/shard_map/dot_general | solution.py:11
  162.7 0.0 reduce-scatter.2.cloned.1.call-update
  162.7 0.0 copy-start.2
  162.7 6.5 %convert_element_type.13 = f32[1024,2048]{1,0:T(8,128)} convert(bf16[1024,2048]{1,0:T(8,128)(2,1)} %param.6) | non-fusion elementwise | flops 2097152 | bytes 12582912 | tf_op jit(solution)/shard_map/convert_element_type | solution.py:19
  169.2 0.6 dynamic-slice
  170.4 2.6 copy.9
  173.0 65.6 %all-reduce = f32[1024]{0:T(1024)S(1)} all-reduce(f32[1024]{0:T(1024)S(1)} %get-tuple-element.6), channel_id=3, replica_groups=mesh['img'=32,'ori'=8] {'img'}, use_global_device_ids=true, to_apply=%region_7.8.clone | all-reduce | flops 1024 | bytes 8192
  238.6 0.1 dynamic-slice_add_fusion
  238.6 80.8 %reduce-scatter.2.cloned.1.call-done = f32[32,2048]{1,0:T(8,128)} async-done(((f32[1024,2048]{1,0:T(8,128)}), f32[32,2048]{1,0:T(8,128)}) %reduce-scatter.2.cloned.1.call-update) | async-done | bytes 262160 | tf_op jit(solution)/shard_map/reduce_scatter | solution.py:44
  319.4 1.8 add_divide_fusion
  (6 shorter events, 0.0 us)
Async XLA Ops:
  7.2 98.7 %copy-start = (f32[1024]{0:T(1024)S(1)}, f32[1024]{0:T(1024)}, u32[]{:S(2)}) copy-start(f32[1024]{0:T(1024)} %param.5) | copy-start | bytes 12292
  7.2 98.4 %all-gather.2.cloned.1.call-start = ((), (), s32[]{:S(2)}) async-start(), calls=%async_computation.1 | async-start | bytes 4718592 | tf_op jit(solution)/shard_map/all_gather | solution.py:18
  9.3 310.1 %reduce-scatter.2.cloned.1.call-start = ((), (), s32[]{:S(2)}) async-start(), calls=%async_computation.2 | async-start | bytes 8650752 | tf_op jit(solution)/shard_map/reduce_scatter | solution.py:44
  152.0 4.0 %copy-start.1 = (bf16[1024,2048]{1,0:T(8,128)(2,1)S(1)}, bf16[1024,2048]{1,0:T(8,128)(2,1)}, u32[]{:S(2)}) copy-start(bf16[1024,2048]{1,0:T(8,128)(2,1)} %all-gather.2.cloned.1.call-done) | copy-start | bytes 12582916
  162.7 6.5 %copy-start.2 = (u32[256]{0:T(256)S(1)}, u32[256]{0:T(256)}, u32[]{:S(2)}) copy-start(u32[256]{0:T(256)} %constant.27) | copy-start | bytes 3076
Sparse Core Ops, SparseCore 0:
  10.3 95.1 all-gather.1
  162.8 156.5 reduce-scatter.1
where the time goes:
time: 328 us
  waiting for transfers between devices  173 us (53%)
  blocking collectives  97.8 us (30%)
  other arithmetic  21.9 us (7%)
  matrix products  16.8 us (5%)
  between operations  14.8 us (5%)
  local copies, waits for them, and re-layouts  3.58 us (1%)
    all_gather x1, waiting for transfers between devices, body(): grouped = lax.all_gather(lowered, 'ori', axis=0, tiled=True)  92.3 us
    reduce_scatter x1, waiting for transfers between devices, body(): lax.psum_scatter(weighted_sums(posteriors, grouped), 'img', scatter_dimen...  80.8 us
    unnamed x1, blocking collectives  65.6 us
    pmax x1, blocking collectives, body(): row_high = lax.pmax(local_high, 'ori')  16.3 us
    psum x1, blocking collectives, body(): row_total = lax.psum(local_total, 'ori')  16 us
    dot_general x1, matrix products, body(): lax.dot_general(grouped, projections, (((1,), (1,)), ((), ())), preferred...  10.2 us
    dot_general x1, matrix products, weighted_sums(): lax.dot_general(weights, rows_block, (((0,), (0,)), ((), ())), preferred_...  6.65 us
  transfers between devices with their start and end apart: 2, of which 2 were waited for; matrix products, arithmetic and copies ran while one was open for 4% of the time, Pallas kernels for 0%

commit v1 on v0

v1 whole, which is shorter than its diff:
```python
import jax
import jax.numpy as jnp
from jax import lax
from jax.experimental import pallas as pl
from jax.experimental.pallas import tpu as pltpu
from jax.sharding import PartitionSpec as P

MESH = pl.DeviceIdType.MESH
prior_weight = 1.0
very_low = -1e30

X_CHIPS, Y_LOW = 4, 2
Z_CHIPS, Y_HIGH, CORES = 8, 2, 2
GROUP = X_CHIPS * Y_LOW
ROWS = 128
DEPTH = 2048
PER = 32
QUARTERS = CORES * Y_HIGH
QROWS = Z_CHIPS * PER
LANES = 128
PIECES = 4
PIECE = ROWS // PIECES
CHUNKS = ((0, 512, True, "z"), (512, 512, False, "z"), (1024, 512, False, "z"), (1536, 512, False, "z"))
STAT_SLOT = {1: 1, 2: 3, 3: 2, 4: 4, 5: 5, 6: 7, 7: 6}

f32 = jnp.float32
bf16 = jnp.bfloat16


def width_of(chunk):
    return chunk[1] + (LANES if chunk[2] else 0)


def kernel(images, precision, projections, tile_mask, posteriors, references, raw, xbuf, table, half_squares, bias, lifted,
           weights, turned, stat_out, stat_in, load_sem, piece_send, piece_recv, stat_send, stat_recv, post_sem,
           core_send, core_recv, ring_send, ring_recv, y_send, y_recv, *chunk_refs):
    img, ori = lax.axis_index("img"), lax.axis_index("ori")
    z, y_hi, core = img // 4, (img // 2) % 2, img % 2
    x, y_lo = ori // 2, ori % 2

    def at_ori(dx, flip):
        row = 1 - y_lo if flip else y_lo
        return ((x + dx) % X_CHIPS) * 2 + row

    where_from = [at_ori(0, False), at_ori(0, True), at_ori(3, False), at_ori(1, False),
                  at_ori(2, False), at_ori(2, True), at_ori(3, True), at_ori(1, True)]
    peers = [(img, w) for w in where_from]
    y_peer, left, right = peers[1], peers[2], peers[3]
    other_core = (z * 4 + y_hi * 2 + 1 - core, ori)
    z_up = (((z + 1) % Z_CHIPS) * 4 + y_hi * 2 + core, ori)
    z_down = (((z + 7) % Z_CHIPS) * 4 + y_hi * 2 + core, ori)
    y_far = (z * 4 + (1 - y_hi) * 2 + core, ori)

    load_images = pltpu.make_async_copy(images, raw, load_sem.at[4])
    load_images.start()
    load_table = []
    for c in range(CORES):
        for yy in range(Y_HIGH):
            q = c * Y_HIGH + yy
            load_table.append(pltpu.make_async_copy(projections.at[:, yy, c], table.at[q], load_sem.at[q]))
            load_table[-1].start()

    barrier = pltpu.get_barrier_semaphore()
    friends = peers[1:] + [other_core, z_up, z_down, y_far]
    for friend in friends:
        pl.semaphore_signal(barrier, inc=1, device_id=friend, device_id_type=MESH)

    load_images.wait()
    xbuf[0] = raw[...].astype(bf16)
    pl.semaphore_wait(barrier, len(friends))

    sends = []
    arrivals = {}
    counter = [0]

    def send_piece(slot, piece, target, far_slot):
        rows = pl.ds(piece * PIECE, PIECE)
        copy = pltpu.make_async_remote_copy(
            src_ref=xbuf.at[slot, rows], dst_ref=xbuf.at[far_slot, rows], send_sem=piece_send.at[counter[0]],
            recv_sem=piece_recv.at[far_slot, piece], device_id=target, device_id_type=MESH)
        counter[0] += 1
        copy.start()
        sends.append(copy)
        arrivals[(far_slot, piece)] = copy

    def arrived(slot, piece):
        arrivals[(slot, piece)].wait_recv()

    half = PIECES // 2
    for i in range(PIECES):
        send_piece(0, i, y_peer, 1)
        send_piece(0, i, right, 2)
        send_piece(0, (i + half) % PIECES, left, 3)

    for copy in load_table:
        copy.wait()

    def square_tile(q, carry):
        wide = table[q].reshape(QROWS, DEPTH).astype(f32)
        total = jnp.sum(wide * wide, axis=1, keepdims=True)
        half_squares[q] = jnp.broadcast_to(0.5 * total, (QROWS, LANES))
        return carry

    lax.fori_loop(0, QUARTERS, square_tile, 0)

    row_ids = lax.broadcasted_iota(jnp.int32, (GROUP, LANES), 0)
    state = {"high": jnp.zeros((GROUP, LANES), f32), "total": jnp.zeros((GROUP, LANES), f32)}

    def score_pair(p):
        slots = (2 * p, 2 * p + 1)
        wide = 2 * LANES
        cols = pl.ds(p * wide, wide)
        for k, slot in enumerate(slots):
            for zz in range(Z_CHIPS):
                live = jnp.where(tile_mask[where_from[slot], zz] > 0, 0.0, very_low)
                bias[pl.ds(zz * PER, PER), pl.ds(k * LANES, LANES)] = jnp.full((PER, LANES), live, f32)
        scale = jnp.concatenate([precision[pl.ds(where_from[slot], 1), :] for slot in slots], axis=1)

        def score_tile(q, high):
            block = table[q].reshape(QROWS, DEPTH)
            rows = xbuf[pl.ds(2 * p, 2)].reshape(wide, DEPTH)
            products = lax.dot_general(block, rows, (((1,), (1,)), ((), ())), preferred_element_type=f32)
            norm = half_squares[q]
            scores = scale * (products - jnp.concatenate([norm, norm], axis=1)) + bias[...]
            lifted[q, :, cols] = scores
            return jnp.maximum(high, jnp.max(scores.reshape(QROWS // 8, 8, wide), axis=0))

        high = lax.fori_loop(0, QUARTERS, score_tile, jnp.full((8, wide), -3e38, f32))
        high = jnp.max(high, axis=0, keepdims=True)

        def lift_tile(q, total):
            values = jnp.exp(lifted[q, :, cols] - high)
            lifted[q, :, cols] = values
            return total + jnp.sum(values.reshape(QROWS // 8, 8, wide), axis=0)

        total = lax.fori_loop(0, QUARTERS, lift_tile, jnp.zeros((8, wide), f32))
        total = jnp.sum(total, axis=0, keepdims=True)
        for k, slot in enumerate(slots):
            here = row_ids == where_from[slot]
            span = slice(k * LANES, (k + 1) * LANES)
            state["high"] = jnp.where(here, high[:, span], state["high"])
            state["total"] = jnp.where(here, total[:, span], state["total"])

    for i in range(half):
        arrived(2, i)
        send_piece(2, i, right, 4)
        arrived(3, half + i)
        send_piece(3, half + i, left, 4)
    for i in range(PIECES):
        arrived(1, i)
        send_piece(1, i, right, 6)
        send_piece(1, i, left, 7)
    score_pair(0)
    for i in range(half):
        arrived(2, half + i)
        arrived(3, i)
    for i in range(half):
        arrived(4, i)
        send_piece(4, i, y_peer, 5)
        arrived(4, half + i)
        send_piece(4, half + i, y_peer, 5)
    score_pair(1)
    for i in range(PIECES):
        arrived(5, i)
    score_pair(2)
    for i in range(PIECES):
        arrived(6, i)
        arrived(7, i)
    score_pair(3)

    my_high, my_total = state["high"], state["total"]
    stat_out[0:GROUP, :] = my_high
    stat_out[GROUP:2 * GROUP, :] = my_total
    stat_copies = []
    for r in range(1, GROUP):
        copy = pltpu.make_async_remote_copy(
            src_ref=stat_out, dst_ref=stat_in.at[STAT_SLOT[r]], send_sem=stat_send.at[r],
            recv_sem=stat_recv.at[STAT_SLOT[r]], device_id=peers[r], device_id_type=MESH)
        copy.start()
        sends.append(copy)
        stat_copies.append(copy)
    for copy in stat_copies:
        copy.wait_recv()
    highest = my_high
    for r in range(1, GROUP):
        highest = jnp.maximum(highest, stat_in[r, 0:GROUP, :])
    my_part = jnp.exp(my_high - highest)
    whole = my_total * my_part
    for r in range(1, GROUP):
        whole = whole + stat_in[r, GROUP:2 * GROUP, :] * jnp.exp(stat_in[r, 0:GROUP, :] - highest)
    factor = my_part / whole
    factor_rows = [jnp.sum(jnp.where(row_ids == w, factor, 0.0), axis=0, keepdims=True) for w in where_from]
    factor_row = jnp.concatenate(factor_rows, axis=1)

    def weight_tile(q, carry):
        weights[q] = (lifted[q] * factor_row).astype(bf16)
        return carry

    lax.fori_loop(0, QUARTERS, weight_tile, 0)

    post_copies = []

    def give_posteriors(slot):
        span = pl.ds(slot * LANES, LANES)

        def tile(zz, carry):
            rows = pl.ds(pl.multiple_of(zz * PER, PER), PER)
            block = jnp.concatenate([lifted[q, rows, span] for q in (0, 2, 1, 3)], axis=0)
            block = (block * factor_rows[slot]).T
            turned[slot, :, pl.ds(pl.multiple_of(zz * LANES, LANES), LANES)] = block.astype(bf16)
            return carry

        lax.fori_loop(0, Z_CHIPS, tile, 0)
        first = pl.multiple_of(where_from[slot] * ROWS, ROWS)
        copy = pltpu.make_async_copy(turned.at[slot], posteriors.at[pl.ds(first, ROWS), :], post_sem.at[slot])
        copy.start()
        post_copies.append(copy)

    per_chunk = [chunk_refs[i * 7:(i + 1) * 7] for i in range(len(CHUNKS))]
    ring_copies = {}
    core_copies, y_copies = {}, {}
    mine_y = core * Y_HIGH

    def product(chunk, q):
        start, wide, counted, _ = chunk
        block = weights[q]
        rows = xbuf[:, :, pl.ds(start, wide)].reshape(GROUP * ROWS, wide)
        value = jnp.dot(block, rows, preferred_element_type=f32)
        if counted:
            ones = jnp.ones((GROUP * ROWS, LANES), bf16)
            value = jnp.concatenate([value, jnp.dot(block, ones, preferred_element_type=f32)], axis=1)
        return value

    def stage_core(j):
        to_core = per_chunk[j][0]

        def one(yy, carry):
            to_core[yy] = product(CHUNKS[j], (1 - core) * Y_HIGH + yy).astype(bf16)
            return carry

        lax.fori_loop(0, Y_HIGH, one, 0)
        copy = pltpu.make_async_remote_copy(
            src_ref=to_core, dst_ref=per_chunk[j][1], send_sem=core_send.at[j], recv_sem=core_recv.at[j],
            device_id=other_core, device_id_type=MESH)
        copy.start()
        sends.append(copy)
        core_copies[j] = copy

    def ring_start(j, step, up, src, dst):
        d = 0 if up else 1
        copy = pltpu.make_async_remote_copy(
            src_ref=src, dst_ref=dst, send_sem=ring_send.at[j, step, d], recv_sem=ring_recv.at[j, step, d],
            device_id=z_up if up else z_down, device_id_type=MESH)
        copy.start()
        sends.append(copy)
        ring_copies[(j, step, d)] = copy

    def ring_first(j):
        local, out, into = per_chunk[j][2], per_chunk[j][3], per_chunk[j][4]
        rows = local.shape[1]
        mid = rows // 2
        far = (z + 4) % Z_CHIPS
        values = local[far].astype(bf16)
        out[0, 0, 0:mid] = values[0:mid]
        out[0, 1, 0:mid] = values[mid:rows]
        for d in range(2):
            ring_start(j, 0, d == 0, out.at[0, d, pl.ds(0, mid)], into.at[0, d, pl.ds(0, mid)])

    def ring_next(j, step):
        local, out, into = per_chunk[j][2], per_chunk[j][3], per_chunk[j][4]
        rows = local.shape[1]
        mid = rows // 2
        for d in range(2):
            ring_copies[(j, step - 1, d)].wait_recv()
            whose = (z + 4 - step) % Z_CHIPS if d == 0 else (z + 4 + step) % Z_CHIPS
            if step == 1:
                got = into[0, d, 0:mid].astype(f32)
                if d == 0:
                    out[1, d, 0:mid] = (local[whose, 0:mid] + got).astype(bf16)
                    out[1, d, mid:rows] = local[whose, mid:rows].astype(bf16)
                else:
                    out[1, d, 0:mid] = local[whose, 0:mid].astype(bf16)
                    out[1, d, mid:rows] = (local[whose, mid:rows] + got).astype(bf16)
            else:
                out[step, d] = (local[whose] + into[step - 1, d].astype(f32)).astype(bf16)
            ring_start(j, step, d == 0, out.at[step, d], into.at[step, d])

    def ring_sum(j):
        local, into = per_chunk[j][2], per_chunk[j][4]
        for d in range(2):
            ring_copies[(j, 3, d)].wait_recv()
        return local[z] + into[3, 0].astype(f32) + into[3, 1].astype(f32)

    def y_start(j):
        copy = pltpu.make_async_remote_copy(
            src_ref=per_chunk[j][5], dst_ref=per_chunk[j][6], send_sem=y_send.at[j], recv_sem=y_recv.at[j],
            device_id=y_far, device_id_type=MESH)
        copy.start()
        sends.append(copy)
        y_copies[j] = copy

    def stage_local(j):
        from_core, local = per_chunk[j][1], per_chunk[j][2]
        wide = width_of(CHUNKS[j])
        z_first = CHUNKS[j][3] == "z"

        def own(yy):
            value = product(CHUNKS[j], mine_y + yy)
            return (value + from_core[yy].astype(f32)).reshape(Z_CHIPS, PER, wide)

        core_copies[j].wait_recv()
        if z_first:
            for yy in range(Y_HIGH):
                local[:, pl.ds(yy * PER, PER), :] = own(yy)
            ring_first(j)
        else:
            per_chunk[j][5][...] = own(1 - y_hi).astype(bf16)
            y_start(j)
            local[...] = own(y_hi)

    state["divide"] = None

    def finish(j, value):
        start, wide, counted, _ = CHUNKS[j]
        if counted:
            state["divide"] = value[:, wide:wide + LANES] + prior_weight
        below = jnp.concatenate([state["divide"]] * (wide // LANES), axis=1)
        prior = table[mine_y + y_hi, z, :, pl.ds(start, wide)].astype(f32)
        references[:, pl.ds(start, wide)] = (value[:, 0:wide] + prior_weight * prior) / below

    def stages(j):
        if CHUNKS[j][3] == "z":
            def to_y():
                local = per_chunk[j][2]
                local[z] = ring_sum(j)
                per_chunk[j][5][...] = local[z, pl.ds(pl.multiple_of((1 - y_hi) * PER, PER), PER), :].astype(bf16)
                y_start(j)

            def last():
                y_copies[j].wait_recv()
                mine = per_chunk[j][2][z, pl.ds(pl.multiple_of(y_hi * PER, PER), PER), :]
                finish(j, mine + per_chunk[j][6][...].astype(f32))

            return [lambda: stage_core(j), lambda: stage_local(j), lambda: ring_next(j, 1), lambda: ring_next(j, 2),
                    lambda: ring_next(j, 3), to_y, last]

        def add_y():
            y_copies[j].wait_recv()
            local = per_chunk[j][2]
            local[...] = local[...] + per_chunk[j][6][...].astype(f32)
            ring_first(j)

        return [lambda: stage_core(j), lambda: stage_local(j), add_y, lambda: ring_next(j, 1), lambda: ring_next(j, 2),
                lambda: ring_next(j, 3), lambda: finish(j, ring_sum(j))]

    plans = [stages(j) for j in range(len(CHUNKS))]
    depth = len(plans[0])
    for t in range(len(CHUNKS) + depth - 1):
        for j in range(len(CHUNKS)):
            s = t - j
            if 0 <= s < depth:
                plans[j][s]()
        if 3 <= t < 7:
            give_posteriors(2 * (t - 3))
            give_posteriors(2 * (t - 3) + 1)

    for copy in sends:
        copy.wait_send()
    for copy in post_copies:
        copy.wait()


def scratch():
    shapes = [
        pltpu.VMEM((ROWS, DEPTH), f32),
        pltpu.VMEM((GROUP, ROWS, DEPTH), bf16),
        pltpu.VMEM((QUARTERS, Z_CHIPS, PER, DEPTH), bf16),
        pltpu.VMEM((QUARTERS, QROWS, LANES), f32),
        pltpu.VMEM((QROWS, 2 * LANES), f32),
        pltpu.VMEM((QUARTERS, QROWS, GROUP * ROWS), f32),
        pltpu.VMEM((QUARTERS, QROWS, GROUP * ROWS), bf16),
        pltpu.VMEM((GROUP, ROWS, QUARTERS * QROWS), bf16),
        pltpu.VMEM((2 * GROUP, LANES), f32),
        pltpu.VMEM((GROUP, 2 * GROUP, LANES), f32),
        pltpu.SemaphoreType.DMA((5,)),
        pltpu.SemaphoreType.DMA((7 * PIECES,)),
        pltpu.SemaphoreType.DMA((GROUP, PIECES)),
        pltpu.SemaphoreType.DMA((GROUP,)),
        pltpu.SemaphoreType.DMA((GROUP,)),
        pltpu.SemaphoreType.DMA((GROUP,)),
        pltpu.SemaphoreType.DMA((len(CHUNKS),)),
        pltpu.SemaphoreType.DMA((len(CHUNKS),)),
        pltpu.SemaphoreType.DMA((len(CHUNKS), 4, 2)),
        pltpu.SemaphoreType.DMA((len(CHUNKS), 4, 2)),
        pltpu.SemaphoreType.DMA((len(CHUNKS),)),
        pltpu.SemaphoreType.DMA((len(CHUNKS),)),
    ]
    for chunk in CHUNKS:
        wide = width_of(chunk)
        z_first = chunk[3] == "z"
        rows = Y_HIGH * PER if z_first else PER
        y_shape = (PER, wide) if z_first else (Z_CHIPS, PER, wide)
        shapes += [
            pltpu.VMEM((Y_HIGH, QROWS, wide), bf16),
            pltpu.VMEM((Y_HIGH, QROWS, wide), bf16),
            pltpu.VMEM((Z_CHIPS, rows, wide), f32),
            pltpu.VMEM((4, 2, rows, wide), bf16),
            pltpu.VMEM((4, 2, rows, wide), bf16),
            pltpu.VMEM(y_shape, bf16),
            pltpu.VMEM(y_shape, bf16),
        ]
    return shapes


def body(images, precision, projections, tile_mask):
    return pl.pallas_call(
        kernel,
        out_shape=(
            jax.ShapeDtypeStruct((GROUP * ROWS, QUARTERS * QROWS), bf16),
            jax.ShapeDtypeStruct((PER, DEPTH), f32),
        ),
        in_specs=[
            pl.BlockSpec(memory_space=pl.ANY),
            pl.BlockSpec(memory_space=pltpu.VMEM),
            pl.BlockSpec(memory_space=pl.ANY),
            pl.BlockSpec(memory_space=pltpu.SMEM),
        ],
        out_specs=(pl.BlockSpec(memory_space=pl.ANY), pl.BlockSpec(memory_space=pltpu.VMEM)),
        scratch_shapes=scratch(),
        compiler_params=pltpu.CompilerParams(
            collective_id=0, has_side_effects=True, vmem_limit_bytes=60 * 1024 * 1024
        ),
    )(images, precision.reshape(GROUP, ROWS), projections.reshape(Z_CHIPS, Y_HIGH, CORES, PER, DEPTH), tile_mask)


def solution(mesh):
    return jax.shard_map(
        body,
        mesh=mesh,
        in_specs=(P(("img", "ori"), None), P("img"), P("ori", None), P("img", "ori")),
        out_specs=(P("img", "ori"), P(("ori", "img"), None)),
        check_vma=False,
    )
```

time: 328 us -> 90.4 us (0.28)
  waiting for transfers between devices: 173 us -> 0 us
  blocking collectives: 97.8 us -> 0 us
  Pallas kernels: 0 us -> 85.7 us
  other arithmetic: 21.9 us -> 0 us
  matrix products: 16.8 us -> 0 us
  between operations: 14.8 us -> 0.65 us
    all_gather x1 -> x0, waiting for transfers between devices: 92.3 us -> none  [body(): grouped = lax.all_gather(lowered, 'ori', axis=0, tiled=True)]
    pallas_call x0 -> x1, Pallas kernels: none -> 85.7 us  [body(): pl.pallas_call(kernel, out_shape=(jax.ShapeDtypeStruct((GROUP * ROWS, QUA...]
    reduce_scatter x1 -> x0, waiting for transfers between devices: 80.8 us -> none  [body(): lax.psum_scatter(weighted_sums(posteriors, grouped), 'img', scatter_dimen...]
    unnamed x1 -> x0, blocking collectives: 65.6 us -> none
    dot_general x2 -> x0, matrix products: 16.8 us -> none  [the longest x1 10.2 us: body(): lax.dot_general(grouped, projections, (((1,), (1,)), ((), ())), preferred...]
    pmax x1 -> x0, blocking collectives: 16.3 us -> none  [body(): row_high = lax.pmax(local_high, 'ori')]
    psum x1 -> x0, blocking collectives: 16 us -> none  [body(): row_total = lax.psum(local_total, 'ori')]
    reduce_sum x3 -> x0, other arithmetic: 10.8 us -> none  [the longest x1 3.99 us: body(): counts = jnp.sum(posteriors.astype(jnp.float32), axis=0)]
  transfers between devices with their start and end apart: 2 -> 0, of which waited for: 2 -> 0; matrix products, arithmetic and copies ran while one was open for 4% -> 0% of each run, Pallas kernels for 0% -> 0%
where the time goes in v1:
time: 90.4 us; the launch traced here: 90.2 us
  Pallas kernels  85.7 us (95%)
  local copies, waits for them, and re-layouts  3.83 us (4%)
    pallas_call x1, Pallas kernels, body(): pl.pallas_call(kernel, out_shape=(jax.ShapeDtypeStruct((GROUP * ROWS, QUA...  85.7 us
    unnamed x4, local copies, waits for them, and re-layouts  3.83 us

profile of v1, /device:TPU:2, one launch (start us, length us, event | category | flops | bytes accessed | tf_op | source)
XLA Modules:
  0.0 90.2 jit_solution(12698610874237799091)
XLA Ops:
  0.6 85.7 %shard_map.59 = (bf16[1024,1024]{1,0:T(8,128)(2,1)}, f32[32,2048]{1,0:T(8,128)}) custom-call(f32[128,2048]{1,0:T(8,128)} %images.1, f32[8,128]{1,0:T(8,128)} %bitcast.3, bf16[8,2,2,32,2048]{4,3,2,1,0:T(8,128)(2,1)} %bitcast.2, s32[8,8]{1,0:T(8,128)} %tile_mask.1), custom_call_target="tpu_custom_call" | custom-call | tf_op jit(solution)/shard_map/pallas_call | solution.py:416
  86.4 0.0 copy-start
  86.4 3.1 %copy.8 = bf16[1024,1024]{1,0:T(8,128)(2,1)} copy(bf16[1024,1024]{1,0:T(8,128)(2,1)} %get-tuple-element.4) | data formatting | bytes 4194304
  89.5 0.0 copy-done
  89.5 0.7 copy.9
Async XLA Ops:
  86.4 3.1 %copy-start = (f32[32,2048]{1,0:T(8,128)S(1)}, f32[32,2048]{1,0:T(8,128)}, u32[]{:S(2)}) copy-start(f32[32,2048]{1,0:T(8,128)} %get-tuple-element.5) | copy-start | bytes 786436

commit v2 on v1

--- a/solution.py
+++ b/solution.py
@@ -12,15 +12,25 @@
 X_CHIPS, Y_LOW = 4, 2
 Z_CHIPS, Y_HIGH, CORES = 8, 2, 2
 GROUP = X_CHIPS * Y_LOW
+HANDS = 8
 ROWS = 128
 DEPTH = 2048
 PER = 32
 QUARTERS = CORES * Y_HIGH
 QROWS = Z_CHIPS * PER
 LANES = 128
-PIECES = 4
-PIECE = ROWS // PIECES
-CHUNKS = ((0, 512, True, "z"), (512, 512, False, "z"), (1024, 512, False, "z"), (1536, 512, False, "z"))
+PIECES = 8
+STACK = 2
+PIECE = DEPTH // PIECES
+PIECE_ORDER = (0, 4, 1, 5, 2, 6, 3, 7)
+CHUNKS = ((0, 256, False, "z"), (256, 256, False, "y"), (512, 256, False, "z"), (768, 256, False, "z"),
+          (1024, 256, True, "y"), (1280, 256, False, "y"), (1536, 256, False, "z"), (1792, 256, False, "z"))
+ORDER = (
+    (0, 0), (1, 0), (2, 0), (3, 0), (4, 0), (0, 1), (1, 1), (2, 1), (5, 0), (3, 1), (6, 0), (0, 2), (4, 1), (2, 2),
+    (5, 1), (6, 1), (3, 2), (7, 0), (0, 3), (1, 2), (2, 3), (7, 1), (6, 2), (3, 3), (0, 4), (1, 3), (2, 4), (7, 2),
+    (4, 2), (6, 3), (3, 4), (0, 5), (1, 4), (2, 5), (5, 2), (7, 3), (4, 3), (6, 4), (0, 6), (3, 5), (1, 5), (5, 3),
+    (2, 6), (7, 4), (4, 4), (6, 5), (1, 6), (5, 4), (3, 6), (7, 5), (4, 5), (5, 5), (6, 6), (4, 6), (7, 6), (5, 6),
+)
 STAT_SLOT = {1: 1, 2: 3, 3: 2, 4: 4, 5: 5, 6: 7, 7: 6}
 
 f32 = jnp.float32
@@ -31,8 +41,8 @@
     return chunk[1] + (LANES if chunk[2] else 0)
 
 
-def kernel(images, precision, projections, tile_mask, posteriors, references, raw, xbuf, table, half_squares, bias, lifted,
-           weights, turned, stat_out, stat_in, load_sem, piece_send, piece_recv, stat_send, stat_recv, post_sem,
+def kernel(images, precision_hbm, projections, mask_hbm, posteriors, references, precision, tile_mask, raw, xbuf, table, half_squares, bias, lifted,
+           weights, turned, given, stat_out, stat_in, load_sem, piece_send, piece_recv, stat_send, stat_recv, post_sem,
            core_send, core_recv, ring_send, ring_recv, y_send, y_recv, *chunk_refs):
     img, ori = lax.axis_index("img"), lax.axis_index("ori")
     z, y_hi, core = img // 4, (img // 2) % 2, img % 2
@@ -51,22 +61,32 @@
     z_down = (((z + 7) % Z_CHIPS) * 4 + y_hi * 2 + core, ori)
     y_far = (z * 4 + (1 - y_hi) * 2 + core, ori)
 
-    load_images = pltpu.make_async_copy(images, raw, load_sem.at[4])
-    load_images.start()
+    load_images = []
+    for i in PIECE_ORDER:
+        span = pl.ds(i * PIECE, PIECE)
+        load_images.append(pltpu.make_async_copy(images.at[:, span], raw.at[:, span], load_sem.at[i]))
+        load_images[-1].start()
+    load_small = [pltpu.make_async_copy(precision_hbm, precision, load_sem.at[PIECES]),
+                  pltpu.make_async_copy(mask_hbm, tile_mask, load_sem.at[PIECES + 1])]
     load_table = []
     for c in range(CORES):
         for yy in range(Y_HIGH):
             q = c * Y_HIGH + yy
-            load_table.append(pltpu.make_async_copy(projections.at[:, yy, c], table.at[q], load_sem.at[q]))
-            load_table[-1].start()
+            load_table.append(
+                pltpu.make_async_copy(projections.at[:, yy, c], table.at[q], load_sem.at[PIECES + 2 + q]))
 
     barrier = pltpu.get_barrier_semaphore()
     friends = peers[1:] + [other_core, z_up, z_down, y_far]
     for friend in friends:
         pl.semaphore_signal(barrier, inc=1, device_id=friend, device_id_type=MESH)
 
-    load_images.wait()
-    xbuf[0] = raw[...].astype(bf16)
+    def lower(place):
+        load_images[place].wait()
+        span = pl.ds(PIECE_ORDER[place] * PIECE, PIECE)
+        xbuf[0, :, span] = raw[:, span].astype(bf16)
+
+    for place in range(2):
+        lower(place)
     pl.semaphore_wait(barrier, len(friends))
 
     sends = []
@@ -74,9 +94,9 @@
     counter = [0]
 
     def send_piece(slot, piece, target, far_slot):
-        rows = pl.ds(piece * PIECE, PIECE)
+        span = pl.ds(piece * PIECE, PIECE)
         copy = pltpu.make_async_remote_copy(
-            src_ref=xbuf.at[slot, rows], dst_ref=xbuf.at[far_slot, rows], send_sem=piece_send.at[counter[0]],
+            src_ref=xbuf.at[slot, :, span], dst_ref=xbuf.at[far_slot, :, span], send_sem=piece_send.at[counter[0]],
             recv_sem=piece_recv.at[far_slot, piece], device_id=target, device_id_type=MESH)
         counter[0] += 1
         copy.start()
@@ -87,12 +107,21 @@
         arrivals[(slot, piece)].wait_recv()
 
     half = PIECES // 2
-    for i in range(PIECES):
+    for i in range(half):
+        if i > 0:
+            lower(2 * i)
+            lower(2 * i + 1)
+        send_piece(0, i, right, 2)
+        send_piece(0, half + i, left, 3)
         send_piece(0, i, y_peer, 1)
-        send_piece(0, i, right, 2)
-        send_piece(0, (i + half) % PIECES, left, 3)
-
-    for copy in load_table:
+        send_piece(0, half + i, y_peer, 1)
+    for i in range(half):
+        send_piece(0, half + i, right, 2)
+        send_piece(0, i, left, 3)
+
+    for copy in load_small + load_table:
+        copy.start()
+    for copy in load_small + load_table:
         copy.wait()
 
     def square_tile(q, carry):
@@ -106,26 +135,49 @@
     row_ids = lax.broadcasted_iota(jnp.int32, (GROUP, LANES), 0)
     state = {"high": jnp.zeros((GROUP, LANES), f32), "total": jnp.zeros((GROUP, LANES), f32)}
 
-    def score_pair(p):
-        slots = (2 * p, 2 * p + 1)
-        wide = 2 * LANES
-        cols = pl.ds(p * wide, wide)
+    def product_tile(q, slots, spans):
+        total = None
+        for first, last in spans:
+            span = pl.ds(first * PIECE, (last - first) * PIECE)
+            block = table[q, :, :, span].reshape(QROWS, (last - first) * PIECE)
+            rows = xbuf[pl.ds(slots[0], len(slots)), :, span].reshape(len(slots) * ROWS, (last - first) * PIECE)
+            part = lax.dot_general(block, rows, (((1,), (1,)), ((), ())), preferred_element_type=f32)
+            total = part if total is None else total + part
+        return total
+
+    def partial_score(slots, spans):
+        cols = pl.ds(slots[0] * LANES, len(slots) * LANES)
+
+        def tile(t, carry):
+            for i in range(STACK):
+                q = t * STACK + i
+                lifted[q, :, cols] = product_tile(q, slots, spans)
+            return carry
+
+        lax.fori_loop(0, QUARTERS // STACK, tile, 0)
+
+    def score(slots, spans=((0, PIECES),), started=False):
+        wide = len(slots) * LANES
+        cols = pl.ds(slots[0] * LANES, wide)
         for k, slot in enumerate(slots):
             for zz in range(Z_CHIPS):
                 live = jnp.where(tile_mask[where_from[slot], zz] > 0, 0.0, very_low)
                 bias[pl.ds(zz * PER, PER), pl.ds(k * LANES, LANES)] = jnp.full((PER, LANES), live, f32)
         scale = jnp.concatenate([precision[pl.ds(where_from[slot], 1), :] for slot in slots], axis=1)
 
-        def score_tile(q, high):
-            block = table[q].reshape(QROWS, DEPTH)
-            rows = xbuf[pl.ds(2 * p, 2)].reshape(wide, DEPTH)
-            products = lax.dot_general(block, rows, (((1,), (1,)), ((), ())), preferred_element_type=f32)
-            norm = half_squares[q]
-            scores = scale * (products - jnp.concatenate([norm, norm], axis=1)) + bias[...]
-            lifted[q, :, cols] = scores
-            return jnp.maximum(high, jnp.max(scores.reshape(QROWS // 8, 8, wide), axis=0))
-
-        high = lax.fori_loop(0, QUARTERS, score_tile, jnp.full((8, wide), -3e38, f32))
+        def score_tile(t, high):
+            for i in range(STACK):
+                q = t * STACK + i
+                products = product_tile(q, slots, spans)
+                if started:
+                    products = products + lifted[q, :, cols]
+                norm = jnp.concatenate([half_squares[q]] * len(slots), axis=1)
+                scores = scale * (products - norm) + bias[:, 0:wide]
+                lifted[q, :, cols] = scores
+                high = jnp.maximum(high, jnp.max(scores.reshape(QROWS // 8, 8, wide), axis=0))
+            return high
+
+        high = lax.fori_loop(0, QUARTERS // STACK, score_tile, jnp.full((8, wide), -3e38, f32))
         high = jnp.max(high, axis=0, keepdims=True)
 
         def lift_tile(q, total):
@@ -141,32 +193,68 @@
             state["high"] = jnp.where(here, high[:, span], state["high"])
             state["total"] = jnp.where(here, total[:, span], state["total"])
 
+    def turn(slot):
+        span = pl.ds(slot * LANES, LANES)
+
+        def tile(zz, carry):
+            rows = pl.ds(pl.multiple_of(zz * PER, PER), PER)
+            block = jnp.concatenate([lifted[q, rows, span] for q in (0, 2, 1, 3)], axis=0)
+            turned[slot, :, pl.ds(pl.multiple_of(zz * LANES, LANES), LANES)] = block.T
+            return carry
+
+        lax.fori_loop(0, Z_CHIPS, tile, 0)
+
     for i in range(half):
         arrived(2, i)
         send_piece(2, i, right, 4)
         arrived(3, half + i)
         send_piece(3, half + i, left, 4)
-    for i in range(PIECES):
+        if i == 1:
+            score((0,))
+    for i in range(half):
         arrived(1, i)
         send_piece(1, i, right, 6)
-        send_piece(1, i, left, 7)
-    score_pair(0)
-    for i in range(half):
+        arrived(1, half + i)
+        send_piece(1, half + i, left, 7)
         arrived(2, half + i)
+        send_piece(2, half + i, y_peer, 6)
         arrived(3, i)
+        send_piece(3, i, y_peer, 7)
+        if i == 0:
+            turn(0)
+    score((1, 2))
+    turn(1)
+    turn(2)
     for i in range(half):
         arrived(4, i)
+        arrived(4, half + i)
+    for i in (half - 1, PIECES - 1):
         send_piece(4, i, y_peer, 5)
-        arrived(4, half + i)
-        send_piece(4, half + i, y_peer, 5)
-    score_pair(1)
-    for i in range(PIECES):
+    for i in range(2):
+        arrived(6, half + i)
+        send_piece(6, half + i, right, 5)
+        arrived(7, i)
+        send_piece(7, i, left, 5)
+    score((3, 4))
+    arrived(6, half + 2)
+    send_piece(6, half + 2, right, 5)
+    arrived(7, 2)
+    send_piece(7, 2, left, 5)
+    turn(3)
+    turn(4)
+    arrived(6, PIECES - 1)
+    arrived(7, half - 1)
+    for i in range(half):
+        arrived(6, i)
+        arrived(7, half + i)
+    score((6, 7))
+    for i in (4, 0, 5, 1, 3):
         arrived(5, i)
-    score_pair(2)
-    for i in range(PIECES):
-        arrived(6, i)
-        arrived(7, i)
-    score_pair(3)
+    partial_score((5,), ((0, 2), (3, 6)))
+    turn(6)
+    for i in (6, 2, 7):
+        arrived(5, i)
+    score((5,), ((2, 3), (6, 8)), True)
 
     my_high, my_total = state["high"], state["total"]
     stat_out[0:GROUP, :] = my_high
@@ -179,6 +267,8 @@
         copy.start()
         sends.append(copy)
         stat_copies.append(copy)
+    for slot in (7, 5):
+        turn(slot)
     for copy in stat_copies:
         copy.wait_recv()
     highest = my_high
@@ -201,18 +291,12 @@
     post_copies = []
 
     def give_posteriors(slot):
-        span = pl.ds(slot * LANES, LANES)
-
-        def tile(zz, carry):
-            rows = pl.ds(pl.multiple_of(zz * PER, PER), PER)
-            block = jnp.concatenate([lifted[q, rows, span] for q in (0, 2, 1, 3)], axis=0)
-            block = (block * factor_rows[slot]).T
-            turned[slot, :, pl.ds(pl.multiple_of(zz * LANES, LANES), LANES)] = block.astype(bf16)
-            return carry
-
-        lax.fori_loop(0, Z_CHIPS, tile, 0)
+        columns = jnp.broadcast_to(factor_rows[slot], (LANES, LANES)).T
+        for t in range(QUARTERS * QROWS // LANES):
+            span = pl.ds(t * LANES, LANES)
+            given[slot, :, span] = (turned[slot, :, span] * columns).astype(bf16)
         first = pl.multiple_of(where_from[slot] * ROWS, ROWS)
-        copy = pltpu.make_async_copy(turned.at[slot], posteriors.at[pl.ds(first, ROWS), :], post_sem.at[slot])
+        copy = pltpu.make_async_copy(given.at[slot], posteriors.at[pl.ds(first, ROWS), :], post_sem.at[slot])
         copy.start()
         post_copies.append(copy)
 
@@ -233,12 +317,8 @@
 
     def stage_core(j):
         to_core = per_chunk[j][0]
-
-        def one(yy, carry):
+        for yy in range(Y_HIGH):
             to_core[yy] = product(CHUNKS[j], (1 - core) * Y_HIGH + yy).astype(bf16)
-            return carry
-
-        lax.fori_loop(0, Y_HIGH, one, 0)
         copy = pltpu.make_async_remote_copy(
             src_ref=to_core, dst_ref=per_chunk[j][1], send_sem=core_send.at[j], recv_sem=core_recv.at[j],
             device_id=other_core, device_id_type=MESH)
@@ -305,8 +385,8 @@
         z_first = CHUNKS[j][3] == "z"
 
         def own(yy):
-            value = product(CHUNKS[j], mine_y + yy)
-            return (value + from_core[yy].astype(f32)).reshape(Z_CHIPS, PER, wide)
+            value = product(CHUNKS[j], mine_y + yy) + from_core[yy].astype(f32)
+            return value.reshape(Z_CHIPS, PER, wide)
 
         core_copies[j].wait_recv()
         if z_first:
@@ -315,18 +395,24 @@
             ring_first(j)
         else:
             per_chunk[j][5][...] = own(1 - y_hi).astype(bf16)
+            local[...] = own(y_hi)
             y_start(j)
-            local[...] = own(y_hi)
 
     state["divide"] = None
+    waiting = []
 
     def finish(j, value):
         start, wide, counted, _ = CHUNKS[j]
         if counted:
             state["divide"] = value[:, wide:wide + LANES] + prior_weight
-        below = jnp.concatenate([state["divide"]] * (wide // LANES), axis=1)
         prior = table[mine_y + y_hi, z, :, pl.ds(start, wide)].astype(f32)
-        references[:, pl.ds(start, wide)] = (value[:, 0:wide] + prior_weight * prior) / below
+        references[:, pl.ds(start, wide)] = value[:, 0:wide] + prior_weight * prior
+        waiting.append((start, wide))
+        if state["divide"] is not None:
+            for first, columns in waiting:
+                below = jnp.concatenate([state["divide"]] * (columns // LANES), axis=1)
+                references[:, pl.ds(first, columns)] = references[:, pl.ds(first, columns)] / below
+            waiting.clear()
 
     def stages(j):
         if CHUNKS[j][3] == "z":
@@ -354,15 +440,10 @@
                 lambda: ring_next(j, 3), lambda: finish(j, ring_sum(j))]
 
     plans = [stages(j) for j in range(len(CHUNKS))]
-    depth = len(plans[0])
-    for t in range(len(CHUNKS) + depth - 1):
-        for j in range(len(CHUNKS)):
-            s = t - j
-            if 0 <= s < depth:
-                plans[j][s]()
-        if 3 <= t < 7:
-            give_posteriors(2 * (t - 3))
-            give_posteriors(2 * (t - 3) + 1)
+    for place, (j, s) in enumerate(ORDER):
+        plans[j][s]()
+        if place % 4 == 3 and place // 4 < GROUP:
+            give_posteriors(place // 4)
 
     for copy in sends:
         copy.wait_send()
@@ -372,6 +453,8 @@
 
 def scratch():
     shapes = [
+        pltpu.VMEM((GROUP, ROWS), f32),
+        pltpu.SMEM((GROUP, Z_CHIPS), jnp.int32),
         pltpu.VMEM((ROWS, DEPTH), f32),
         pltpu.VMEM((GROUP, ROWS, DEPTH), bf16),
         pltpu.VMEM((QUARTERS, Z_CHIPS, PER, DEPTH), bf16),
@@ -379,10 +462,11 @@
         pltpu.VMEM((QROWS, 2 * LANES), f32),
         pltpu.VMEM((QUARTERS, QROWS, GROUP * ROWS), f32),
         pltpu.VMEM((QUARTERS, QROWS, GROUP * ROWS), bf16),
+        pltpu.VMEM((GROUP, ROWS, QUARTERS * QROWS), f32),
         pltpu.VMEM((GROUP, ROWS, QUARTERS * QROWS), bf16),
         pltpu.VMEM((2 * GROUP, LANES), f32),
         pltpu.VMEM((GROUP, 2 * GROUP, LANES), f32),
-        pltpu.SemaphoreType.DMA((5,)),
+        pltpu.SemaphoreType.DMA((PIECES + 2 + QUARTERS,)),
         pltpu.SemaphoreType.DMA((7 * PIECES,)),
         pltpu.SemaphoreType.DMA((GROUP, PIECES)),
         pltpu.SemaphoreType.DMA((GROUP,)),
@@ -412,25 +496,44 @@
     return shapes
 
 
+def hand_over(posts, refs, posts_out, refs_out, sem):
+    rows = GROUP * ROWS // HANDS
+    spans = [pl.ds(i * rows, rows) for i in range(HANDS)]
+    copies = [pltpu.make_async_copy(posts.at[s], posts_out.at[s], sem.at[i]) for i, s in enumerate(spans)]
+    copies.append(pltpu.make_async_copy(refs, refs_out, sem.at[HANDS]))
+    for copy in copies:
+        copy.start()
+    for copy in copies:
+        copy.wait()
+
+
 def body(images, precision, projections, tile_mask):
-    return pl.pallas_call(
+    posts, refs = pl.pallas_call(
         kernel,
         out_shape=(
             jax.ShapeDtypeStruct((GROUP * ROWS, QUARTERS * QROWS), bf16),
             jax.ShapeDtypeStruct((PER, DEPTH), f32),
         ),
         in_specs=[
-            pl.BlockSpec(memory_space=pl.ANY),
-            pl.BlockSpec(memory_space=pltpu.VMEM),
-            pl.BlockSpec(memory_space=pl.ANY),
-            pl.BlockSpec(memory_space=pltpu.SMEM),
+            pl.BlockSpec(memory_space=pltpu.HBM),
+            pl.BlockSpec(memory_space=pltpu.HBM),
+            pl.BlockSpec(memory_space=pltpu.HBM),
+            pl.BlockSpec(memory_space=pltpu.HBM),
         ],
         out_specs=(pl.BlockSpec(memory_space=pl.ANY), pl.BlockSpec(memory_space=pltpu.VMEM)),
         scratch_shapes=scratch(),
         compiler_params=pltpu.CompilerParams(
-            collective_id=0, has_side_effects=True, vmem_limit_bytes=60 * 1024 * 1024
+            collective_id=0, has_side_effects=True, vmem_limit_bytes=40 * 1024 * 1024
         ),
-    )(images, precision.reshape(GROUP, ROWS), projections.reshape(Z_CHIPS, Y_HIGH, CORES, PER, DEPTH), tile_mask)
+    )(*[pltpu.with_memory_space_constraint(v, pltpu.HBM) for v in (images, precision.reshape(GROUP, ROWS), projections.reshape(Z_CHIPS, Y_HIGH, CORES, PER, DEPTH), tile_mask)])
+    return pl.pallas_call(
+        hand_over,
+        out_shape=(jax.ShapeDtypeStruct(posts.shape, bf16), jax.ShapeDtypeStruct(refs.shape, f32)),
+        in_specs=[pl.BlockSpec(memory_space=pl.ANY)] * 2,
+        out_specs=(pl.BlockSpec(memory_space=pltpu.HBM), pl.BlockSpec(memory_space=pltpu.HBM)),
+        scratch_shapes=[pltpu.SemaphoreType.DMA((HANDS + 1,))],
+        compiler_params=pltpu.CompilerParams(vmem_limit_bytes=4 * 1024 * 1024),
+    )(posts, refs)
 
 
 def solution(mesh):

time: 90.4 us -> 78.8 us (0.87)
  Pallas kernels: 85.7 us -> 77.7 us
  local copies, waits for them, and re-layouts: 3.83 us -> 0 us
    pallas_call x1, Pallas kernels: 85.7 us -> 76.2 us  [body(): pl.pallas_call(kernel, out_shape=(jax.ShapeDtypeStruct((GROUP * ROWS, QUA...]
    unnamed x4 -> x0, local copies, waits for them, and re-layouts: 3.83 us -> none
    pallas_call x0 -> x1, Pallas kernels: none -> 1.47 us  [body(): pl.pallas_call(hand_over, out_shape=(jax.ShapeDtypeStruct(posts.shape, bf...]
where the time goes in v2:
time: 78.8 us; the launch traced here: 78.3 us
  Pallas kernels  77.7 us (99%)
    pallas_call x1, Pallas kernels, body(): pl.pallas_call(kernel, out_shape=(jax.ShapeDtypeStruct((GROUP * ROWS, QUA...  76.2 us

profile of v2, /device:TPU:2, one launch (start us, length us, event | category | flops | bytes accessed | tf_op | source)
XLA Modules:
  0.0 78.3 jit_solution(6285536793041611619)
XLA Ops:
  0.6 76.2 %shard_map.59 = (bf16[1024,1024]{1,0:T(8,128)(2,1)S(1)}, f32[32,2048]{1,0:T(8,128)S(1)}) custom-call(f32[128,2048]{1,0:T(8,128)} %images.1, f32[8,128]{1,0:T(8,128)} %bitcast.3, bf16[8,2,2,32,2048]{4,3,2,1,0:T(8,128)(2,1)} %bitcast.2, s32[8,8]{1,0:T(8,128)} %mask_hbm.1), custom_call_target="tpu_custom_call" | custom-call | tf_op jit(solution)/shard_map/pallas_call | solution.py:511
  76.8 1.5 %shard_map.60 = (bf16[1024,1024]{1,0:T(8,128)(2,1)}, f32[32,2048]{1,0:T(8,128)}) custom-call(bf16[1024,1024]{1,0:T(8,128)(2,1)S(1)} %get-tuple-element.4.posts, f32[32,2048]{1,0:T(8,128)S(1)} %get-tuple-element.5.refs), custom_call_target="tpu_custom_call" | custom-call | tf_op jit(solution)/shard_map/pallas_call | solution.py:529

commit v3 on v2

--- a/solution.py
+++ b/solution.py
@@ -23,13 +23,22 @@
 STACK = 2
 PIECE = DEPTH // PIECES
 PIECE_ORDER = (0, 4, 1, 5, 2, 6, 3, 7)
-CHUNKS = ((0, 256, False, "z"), (256, 256, False, "y"), (512, 256, False, "z"), (768, 256, False, "z"),
-          (1024, 256, True, "y"), (1280, 256, False, "y"), (1536, 256, False, "z"), (1792, 256, False, "z"))
+CHUNKS = (
+    (0, 256, False, "z"),
+    (256, 256, False, "z"),
+    (512, 256, False, "y"),
+    (768, 256, True, "y"),
+    (1024, 256, False, "z"),
+    (1280, 256, False, "y"),
+    (1536, 256, False, "z"),
+    (1792, 256, False, "y"),
+)
 ORDER = (
-    (0, 0), (1, 0), (2, 0), (3, 0), (4, 0), (0, 1), (1, 1), (2, 1), (5, 0), (3, 1), (6, 0), (0, 2), (4, 1), (2, 2),
-    (5, 1), (6, 1), (3, 2), (7, 0), (0, 3), (1, 2), (2, 3), (7, 1), (6, 2), (3, 3), (0, 4), (1, 3), (2, 4), (7, 2),
-    (4, 2), (6, 3), (3, 4), (0, 5), (1, 4), (2, 5), (5, 2), (7, 3), (4, 3), (6, 4), (0, 6), (3, 5), (1, 5), (5, 3),
-    (2, 6), (7, 4), (4, 4), (6, 5), (1, 6), (5, 4), (3, 6), (7, 5), (4, 5), (5, 5), (6, 6), (4, 6), (7, 6), (5, 6),
+    (0, 0), (1, 0), (2, 0), (3, 0), (4, 0), (5, 0), (6, 0), (0, 1), (1, 1), (2, 1), (7, 0), (3, 1),
+    (4, 1), (5, 1), (0, 2), (6, 1), (1, 2), (7, 1), (7, 2), (3, 2), (5, 2), (2, 2), (2, 3), (4, 2),
+    (3, 3), (0, 3), (6, 2), (1, 3), (5, 3), (2, 4), (7, 3), (4, 3), (3, 4), (0, 4), (6, 3), (1, 4),
+    (5, 4), (7, 4), (4, 4), (3, 5), (0, 5), (6, 4), (1, 5), (5, 5), (7, 5), (2, 5), (4, 5), (3, 6),
+    (0, 6), (6, 5), (5, 6), (7, 6), (1, 6), (2, 6), (3, 7), (4, 6), (5, 7), (6, 6), (7, 7), (2, 7),
 )
 STAT_SLOT = {1: 1, 2: 3, 3: 2, 4: 4, 5: 5, 6: 7, 7: 6}
 
@@ -251,7 +260,6 @@
     for i in (4, 0, 5, 1, 3):
         arrived(5, i)
     partial_score((5,), ((0, 2), (3, 6)))
-    turn(6)
     for i in (6, 2, 7):
         arrived(5, i)
     score((5,), ((2, 3), (6, 8)), True)
@@ -267,7 +275,7 @@
         copy.start()
         sends.append(copy)
         stat_copies.append(copy)
-    for slot in (7, 5):
+    for slot in (6, 7, 5):
         turn(slot)
     for copy in stat_copies:
         copy.wait_recv()
@@ -336,48 +344,65 @@
         ring_copies[(j, step, d)] = copy
 
     def ring_first(j):
-        local, out, into = per_chunk[j][2], per_chunk[j][3], per_chunk[j][4]
-        rows = local.shape[1]
+        out, into = per_chunk[j][3], per_chunk[j][4]
+        rows = out.shape[2]
         mid = rows // 2
-        far = (z + 4) % Z_CHIPS
-        values = local[far].astype(bf16)
+        values = local_rows(j, 4).astype(bf16)
         out[0, 0, 0:mid] = values[0:mid]
         out[0, 1, 0:mid] = values[mid:rows]
         for d in range(2):
             ring_start(j, 0, d == 0, out.at[0, d, pl.ds(0, mid)], into.at[0, d, pl.ds(0, mid)])
 
     def ring_next(j, step):
-        local, out, into = per_chunk[j][2], per_chunk[j][3], per_chunk[j][4]
-        rows = local.shape[1]
+        out, into = per_chunk[j][3], per_chunk[j][4]
+        rows = out.shape[2]
         mid = rows // 2
         for d in range(2):
+            mine = local_rows(j, 4 - step if d == 0 else 4 + step)
             ring_copies[(j, step - 1, d)].wait_recv()
-            whose = (z + 4 - step) % Z_CHIPS if d == 0 else (z + 4 + step) % Z_CHIPS
             if step == 1:
                 got = into[0, d, 0:mid].astype(f32)
                 if d == 0:
-                    out[1, d, 0:mid] = (local[whose, 0:mid] + got).astype(bf16)
-                    out[1, d, mid:rows] = local[whose, mid:rows].astype(bf16)
+                    out[1, d, 0:mid] = (mine[0:mid] + got).astype(bf16)
+                    out[1, d, mid:rows] = mine[mid:rows].astype(bf16)
                 else:
-                    out[1, d, 0:mid] = local[whose, 0:mid].astype(bf16)
-                    out[1, d, mid:rows] = (local[whose, mid:rows] + got).astype(bf16)
+                    out[1, d, 0:mid] = mine[0:mid].astype(bf16)
+                    out[1, d, mid:rows] = (mine[mid:rows] + got).astype(bf16)
             else:
-                out[step, d] = (local[whose] + into[step - 1, d].astype(f32)).astype(bf16)
+                out[step, d] = (mine + into[step - 1, d].astype(f32)).astype(bf16)
             ring_start(j, step, d == 0, out.at[step, d], into.at[step, d])
 
     def ring_sum(j):
-        local, into = per_chunk[j][2], per_chunk[j][4]
+        into = per_chunk[j][4]
+        mine = local_rows(j, 0)
         for d in range(2):
             ring_copies[(j, 3, d)].wait_recv()
-        return local[z] + into[3, 0].astype(f32) + into[3, 1].astype(f32)
+        return mine + into[3, 0].astype(f32) + into[3, 1].astype(f32)
 
     def y_start(j):
         copy = pltpu.make_async_remote_copy(
-            src_ref=per_chunk[j][5], dst_ref=per_chunk[j][6], send_sem=y_send.at[j], recv_sem=y_recv.at[j],
+            src_ref=per_chunk[j][5], dst_ref=per_chunk[j][6], send_sem=y_send.at[j, 0], recv_sem=y_recv.at[j, 0],
             device_id=y_far, device_id_type=MESH)
         copy.start()
         sends.append(copy)
         y_copies[j] = copy
+
+    def y_slices(j, steps):
+        for step in steps:
+            which = (z + step) % Z_CHIPS
+            copy = pltpu.make_async_remote_copy(
+                src_ref=per_chunk[j][5].at[which], dst_ref=per_chunk[j][6].at[which], send_sem=y_send.at[j, step],
+                recv_sem=y_recv.at[j, step], device_id=y_far, device_id_type=MESH)
+            copy.start()
+            sends.append(copy)
+            y_copies[(j, step)] = copy
+
+    def local_rows(j, step):
+        which = (z + step) % Z_CHIPS
+        if CHUNKS[j][3] == "z":
+            return per_chunk[j][2][which]
+        y_copies[(j, step)].wait_recv()
+        return per_chunk[j][2][which] + per_chunk[j][6][which].astype(f32)
 
     def stage_local(j):
         from_core, local = per_chunk[j][1], per_chunk[j][2]
@@ -396,7 +421,7 @@
         else:
             per_chunk[j][5][...] = own(1 - y_hi).astype(bf16)
             local[...] = own(y_hi)
-            y_start(j)
+            y_slices(j, (4, 3, 5))
 
     state["divide"] = None
     waiting = []
@@ -430,14 +455,8 @@
             return [lambda: stage_core(j), lambda: stage_local(j), lambda: ring_next(j, 1), lambda: ring_next(j, 2),
                     lambda: ring_next(j, 3), to_y, last]
 
-        def add_y():
-            y_copies[j].wait_recv()
-            local = per_chunk[j][2]
-            local[...] = local[...] + per_chunk[j][6][...].astype(f32)
-            ring_first(j)
-
-        return [lambda: stage_core(j), lambda: stage_local(j), add_y, lambda: ring_next(j, 1), lambda: ring_next(j, 2),
-                lambda: ring_next(j, 3), lambda: finish(j, ring_sum(j))]
+        return [lambda: stage_core(j), lambda: stage_local(j), lambda: y_slices(j, (2, 6, 1, 7, 0)), lambda: ring_first(j),
+                lambda: ring_next(j, 1), lambda: ring_next(j, 2), lambda: ring_next(j, 3), lambda: finish(j, ring_sum(j))]
 
     plans = [stages(j) for j in range(len(CHUNKS))]
     for place, (j, s) in enumerate(ORDER):
@@ -476,8 +495,8 @@
         pltpu.SemaphoreType.DMA((len(CHUNKS),)),
         pltpu.SemaphoreType.DMA((len(CHUNKS), 4, 2)),
         pltpu.SemaphoreType.DMA((len(CHUNKS), 4, 2)),
-        pltpu.SemaphoreType.DMA((len(CHUNKS),)),
-        pltpu.SemaphoreType.DMA((len(CHUNKS),)),
+        pltpu.SemaphoreType.DMA((len(CHUNKS), Z_CHIPS)),
+        pltpu.SemaphoreType.DMA((len(CHUNKS), Z_CHIPS)),
     ]
     for chunk in CHUNKS:
         wide = width_of(chunk)

time: 78.8 us -> 76.1 us (0.966)
  Pallas kernels: 77.7 us -> 75.4 us
    pallas_call x1, Pallas kernels: 76.2 us -> 73.9 us  [body(): pl.pallas_call(kernel, out_shape=(jax.ShapeDtypeStruct((GROUP * ROWS, QUA...]
where the time goes in v3:
time: 76.1 us; the launch traced here: 76 us
  Pallas kernels  75.4 us (99%)
    pallas_call x1, Pallas kernels, body(): pl.pallas_call(kernel, out_shape=(jax.ShapeDtypeStruct((GROUP * ROWS, QUA...  73.9 us

profile of v3, /device:TPU:2, one launch (start us, length us, event | category | flops | bytes accessed | tf_op | source)
XLA Modules:
  0.0 76.0 jit_solution(11873936789277902180)
XLA Ops:
  0.6 73.9 %shard_map.59 = (bf16[1024,1024]{1,0:T(8,128)(2,1)S(1)}, f32[32,2048]{1,0:T(8,128)S(1)}) custom-call(f32[128,2048]{1,0:T(8,128)} %images.1, f32[8,128]{1,0:T(8,128)} %bitcast.3, bf16[8,2,2,32,2048]{4,3,2,1,0:T(8,128)(2,1)} %bitcast.2, s32[8,8]{1,0:T(8,128)} %mask_hbm.1), custom_call_target="tpu_custom_call" | custom-call | tf_op jit(solution)/shard_map/pallas_call | solution.py:530
  74.6 1.5 %shard_map.60 = (bf16[1024,1024]{1,0:T(8,128)(2,1)}, f32[32,2048]{1,0:T(8,128)}) custom-call(bf16[1024,1024]{1,0:T(8,128)(2,1)S(1)} %get-tuple-element.4.posts, f32[32,2048]{1,0:T(8,128)S(1)} %get-tuple-element.5.refs), custom_call_target="tpu_custom_call" | custom-call | tf_op jit(solution)/shard_map/pallas_call | solution.py:548

commit v4 on v3

--- a/solution.py
+++ b/solution.py
@@ -51,7 +51,7 @@
 
 
 def kernel(images, precision_hbm, projections, mask_hbm, posteriors, references, precision, tile_mask, raw, xbuf, table, half_squares, bias, lifted,
-           weights, turned, given, stat_out, stat_in, load_sem, piece_send, piece_recv, stat_send, stat_recv, post_sem,
+           weights, turned, given, stat_out, stat_in, ready, load_sem, piece_send, piece_recv, stat_send, stat_recv, post_sem,
            core_send, core_recv, ring_send, ring_recv, y_send, y_recv, *chunk_refs):
     img, ori = lax.axis_index("img"), lax.axis_index("ori")
     z, y_hi, core = img // 4, (img // 2) % 2, img % 2
@@ -85,7 +85,12 @@
                 pltpu.make_async_copy(projections.at[:, yy, c], table.at[q], load_sem.at[PIECES + 2 + q]))
 
     barrier = pltpu.get_barrier_semaphore()
-    friends = peers[1:] + [other_core, z_up, z_down, y_far]
+    y = y_hi * Y_LOW + y_lo
+    y_sides = []
+    for step in (1, 3):
+        there = (y + step) % (Y_HIGH * Y_LOW)
+        y_sides.append((z * 4 + (there // Y_LOW) * 2 + core, x * 2 + there % Y_LOW))
+    friends = y_sides + [left, right, other_core, z_up, z_down]
     for friend in friends:
         pl.semaphore_signal(barrier, inc=1, device_id=friend, device_id_type=MESH)
 
@@ -97,6 +102,8 @@
     for place in range(2):
         lower(place)
     pl.semaphore_wait(barrier, len(friends))
+    for side in y_sides:
+        pl.semaphore_signal(ready, inc=1, device_id=side, device_id_type=MESH)
 
     sends = []
     arrivals = {}
@@ -458,6 +465,7 @@
         return [lambda: stage_core(j), lambda: stage_local(j), lambda: y_slices(j, (2, 6, 1, 7, 0)), lambda: ring_first(j),
                 lambda: ring_next(j, 1), lambda: ring_next(j, 2), lambda: ring_next(j, 3), lambda: finish(j, ring_sum(j))]
 
+    pl.semaphore_wait(ready, 2)
     plans = [stages(j) for j in range(len(CHUNKS))]
     for place, (j, s) in enumerate(ORDER):
         plans[j][s]()
@@ -485,6 +493,7 @@
         pltpu.VMEM((GROUP, ROWS, QUARTERS * QROWS), bf16),
         pltpu.VMEM((2 * GROUP, LANES), f32),
         pltpu.VMEM((GROUP, 2 * GROUP, LANES), f32),
+        pltpu.SemaphoreType.REGULAR,
         pltpu.SemaphoreType.DMA((PIECES + 2 + QUARTERS,)),
         pltpu.SemaphoreType.DMA((7 * PIECES,)),
         pltpu.SemaphoreType.DMA((GROUP, PIECES)),

time: 76.1 us -> 75.7 us (level)
  no operation moved by 1% of the time
where the time goes in v4:
time: 75.7 us; the launch traced here: 75.6 us
  Pallas kernels  75 us (99%)
    pallas_call x1, Pallas kernels, body(): pl.pallas_call(kernel, out_shape=(jax.ShapeDtypeStruct((GROUP * ROWS, QUA...  73.5 us

profile of v4, /device:TPU:2, one launch (start us, length us, event | category | flops | bytes accessed | tf_op | source)
XLA Modules:
  0.0 75.6 jit_solution(12557369932089564717)
XLA Ops:
  0.6 73.5 %shard_map.59 = (bf16[1024,1024]{1,0:T(8,128)(2,1)S(1)}, f32[32,2048]{1,0:T(8,128)S(1)}) custom-call(f32[128,2048]{1,0:T(8,128)} %images.1, f32[8,128]{1,0:T(8,128)} %bitcast.3, bf16[8,2,2,32,2048]{4,3,2,1,0:T(8,128)(2,1)} %bitcast.2, s32[8,8]{1,0:T(8,128)} %mask_hbm.1), custom_call_target="tpu_custom_call" | custom-call | tf_op jit(solution)/shard_map/pallas_call | solution.py:539
  74.1 1.5 %shard_map.60 = (bf16[1024,1024]{1,0:T(8,128)(2,1)}, f32[32,2048]{1,0:T(8,128)}) custom-call(bf16[1024,1024]{1,0:T(8,128)(2,1)S(1)} %get-tuple-element.4.posts, f32[32,2048]{1,0:T(8,128)S(1)} %get-tuple-element.5.refs), custom_call_target="tpu_custom_call" | custom-call | tf_op jit(solution)/shard_map/pallas_call | solution.py:557

commit v5 on v4

--- a/solution.py
+++ b/solution.py
@@ -244,7 +244,7 @@
     for i in range(half):
         arrived(4, i)
         arrived(4, half + i)
-    for i in (half - 1, PIECES - 1):
+    for i in (3, 6, 7):
         send_piece(4, i, y_peer, 5)
     for i in range(2):
         arrived(6, half + i)
@@ -253,7 +253,6 @@
         send_piece(7, i, left, 5)
     score((3, 4))
     arrived(6, half + 2)
-    send_piece(6, half + 2, right, 5)
     arrived(7, 2)
     send_piece(7, 2, left, 5)
     turn(3)

time: 75.7 us -> 75.7 us (level)
  no operation moved by 1% of the time
where the time goes in v5:
time: 75.7 us; the launch traced here: 75.6 us
  Pallas kernels  75 us (99%)
    pallas_call x1, Pallas kernels, body(): pl.pallas_call(kernel, out_shape=(jax.ShapeDtypeStruct((GROUP * ROWS, QUA...  73.5 us

profile of v5, /device:TPU:2, one launch (start us, length us, event | category | flops | bytes accessed | tf_op | source)
XLA Modules:
  0.0 75.6 jit_solution(14333453176685254207)
XLA Ops:
  0.6 73.5 %shard_map.59 = (bf16[1024,1024]{1,0:T(8,128)(2,1)S(1)}, f32[32,2048]{1,0:T(8,128)S(1)}) custom-call(f32[128,2048]{1,0:T(8,128)} %images.1, f32[8,128]{1,0:T(8,128)} %bitcast.3, bf16[8,2,2,32,2048]{4,3,2,1,0:T(8,128)(2,1)} %bitcast.2, s32[8,8]{1,0:T(8,128)} %mask_hbm.1), custom_call_target="tpu_custom_call" | custom-call | tf_op jit(solution)/shard_map/pallas_call | solution.py:538
  74.1 1.5 %shard_map.60 = (bf16[1024,1024]{1,0:T(8,128)(2,1)}, f32[32,2048]{1,0:T(8,128)}) custom-call(bf16[1024,1024]{1,0:T(8,128)(2,1)S(1)} %get-tuple-element.4.posts, f32[32,2048]{1,0:T(8,128)S(1)} %get-tuple-element.5.refs), custom_call_target="tpu_custom_call" | custom-call | tf_op jit(solution)/shard_map/pallas_call | solution.py:556

commit v6 on v5

--- a/solution.py
+++ b/solution.py
@@ -12,7 +12,7 @@
 X_CHIPS, Y_LOW = 4, 2
 Z_CHIPS, Y_HIGH, CORES = 8, 2, 2
 GROUP = X_CHIPS * Y_LOW
-HANDS = 8
+HANDS = 2
 ROWS = 128
 DEPTH = 2048
 PER = 32
@@ -263,12 +263,12 @@
         arrived(6, i)
         arrived(7, half + i)
     score((6, 7))
-    for i in (4, 0, 5, 1, 3):
+    for i in (4, 0, 5, 1, 3, 6):
         arrived(5, i)
-    partial_score((5,), ((0, 2), (3, 6)))
-    for i in (6, 2, 7):
+    partial_score((5,), ((0, 2), (3, 7)))
+    for i in (2, 7):
         arrived(5, i)
-    score((5,), ((2, 3), (6, 8)), True)
+    score((5,), ((2, 3), (7, 8)), True)
 
     my_high, my_total = state["high"], state["total"]
     stat_out[0:GROUP, :] = my_high
@@ -300,7 +300,7 @@
         weights[q] = (lifted[q] * factor_row).astype(bf16)
         return carry
 
-    lax.fori_loop(0, QUARTERS, weight_tile, 0)
+    lax.fori_loop((1 - core) * Y_HIGH, (1 - core) * Y_HIGH + Y_HIGH, weight_tile, 0)
 
     post_copies = []
 
@@ -468,6 +468,8 @@
     plans = [stages(j) for j in range(len(CHUNKS))]
     for place, (j, s) in enumerate(ORDER):
         plans[j][s]()
+        if place == 0:
+            lax.fori_loop(core * Y_HIGH, core * Y_HIGH + Y_HIGH, weight_tile, 0)
         if place % 4 == 3 and place // 4 < GROUP:
             give_posteriors(place // 4)
 

time: 75.7 us -> 75.9 us (level)
  no operation moved by 1% of the time
where the time goes in v6:
time: 75.9 us; the launch traced here: 75.8 us
  Pallas kernels  75 us (99%)
  between operations  0.8 us (1%)
    pallas_call x1, Pallas kernels, body(): pl.pallas_call(kernel, out_shape=(jax.ShapeDtypeStruct((GROUP * ROWS, QUA...  73.5 us

profile of v6, /device:TPU:2, one launch (start us, length us, event | category | flops | bytes accessed | tf_op | source)
XLA Modules:
  0.0 75.8 jit_solution(17620468646229101141)
XLA Ops:
  0.6 73.5 %shard_map.59 = (bf16[1024,1024]{1,0:T(8,128)(2,1)S(1)}, f32[32,2048]{1,0:T(8,128)S(1)}) custom-call(f32[128,2048]{1,0:T(8,128)} %images.1, f32[8,128]{1,0:T(8,128)} %bitcast.3, bf16[8,2,2,32,2048]{4,3,2,1,0:T(8,128)(2,1)} %bitcast.2, s32[8,8]{1,0:T(8,128)} %mask_hbm.1), custom_call_target="tpu_custom_call" | custom-call | tf_op jit(solution)/shard_map/pallas_call | solution.py:540
  74.2 1.4 %shard_map.60 = (bf16[1024,1024]{1,0:T(8,128)(2,1)}, f32[32,2048]{1,0:T(8,128)}) custom-call(bf16[1024,1024]{1,0:T(8,128)(2,1)S(1)} %get-tuple-element.4.posts, f32[32,2048]{1,0:T(8,128)S(1)} %get-tuple-element.5.refs), custom_call_target="tpu_custom_call" | custom-call | tf_op jit(solution)/shard_map/pallas_call | solution.py:558

commit v7 on v6

--- a/solution.py
+++ b/solution.py
@@ -34,11 +34,11 @@
     (1792, 256, False, "y"),
 )
 ORDER = (
-    (0, 0), (1, 0), (2, 0), (3, 0), (4, 0), (5, 0), (6, 0), (0, 1), (1, 1), (2, 1), (7, 0), (3, 1),
-    (4, 1), (5, 1), (0, 2), (6, 1), (1, 2), (7, 1), (7, 2), (3, 2), (5, 2), (2, 2), (2, 3), (4, 2),
-    (3, 3), (0, 3), (6, 2), (1, 3), (5, 3), (2, 4), (7, 3), (4, 3), (3, 4), (0, 4), (6, 3), (1, 4),
-    (5, 4), (7, 4), (4, 4), (3, 5), (0, 5), (6, 4), (1, 5), (5, 5), (7, 5), (2, 5), (4, 5), (3, 6),
-    (0, 6), (6, 5), (5, 6), (7, 6), (1, 6), (2, 6), (3, 7), (4, 6), (5, 7), (6, 6), (7, 7), (2, 7),
+    (1, 0), (2, 0), (0, 0), (4, 0), (6, 0), (5, 0), (3, 0), (1, 1), (2, 1), (0, 1), (2, 2), (4, 1),
+    (7, 0), (6, 1), (1, 2), (5, 1), (0, 2), (3, 1), (4, 2), (2, 3), (6, 2), (7, 1), (1, 3), (0, 3),
+    (5, 2), (3, 2), (4, 3), (2, 4), (5, 3), (3, 3), (6, 3), (7, 2), (7, 3), (1, 4), (4, 4), (3, 4),
+    (5, 4), (7, 4), (6, 4), (2, 5), (0, 4), (3, 5), (5, 5), (1, 5), (7, 5), (4, 5), (2, 6), (0, 5),
+    (6, 5), (3, 6), (5, 6), (7, 6), (4, 6), (2, 7), (0, 6), (6, 6), (1, 6), (5, 7), (3, 7), (7, 7),
 )
 STAT_SLOT = {1: 1, 2: 3, 3: 2, 4: 4, 5: 5, 6: 7, 7: 6}
 

time: 75.9 us -> 75.7 us (level)
  no operation moved by 1% of the time
where the time goes in v7:
time: 75.7 us; the launch traced here: 75.3 us
  Pallas kernels  74.5 us (98%)
  between operations  0.8 us (1%)
    pallas_call x1, Pallas kernels, body(): pl.pallas_call(kernel, out_shape=(jax.ShapeDtypeStruct((GROUP * ROWS, QUA...  73 us

profile of v7, /device:TPU:2, one launch (start us, length us, event | category | flops | bytes accessed | tf_op | source)
XLA Modules:
  0.0 75.3 jit_solution(16260488383018195694)
XLA Ops:
  0.6 73.0 %shard_map.59 = (bf16[1024,1024]{1,0:T(8,128)(2,1)S(1)}, f32[32,2048]{1,0:T(8,128)S(1)}) custom-call(f32[128,2048]{1,0:T(8,128)} %images.1, f32[8,128]{1,0:T(8,128)} %bitcast.3, bf16[8,2,2,32,2048]{4,3,2,1,0:T(8,128)(2,1)} %bitcast.2, s32[8,8]{1,0:T(8,128)} %mask_hbm.1), custom_call_target="tpu_custom_call" | custom-call | tf_op jit(solution)/shard_map/pallas_call | solution.py:540
  73.7 1.4 %shard_map.60 = (bf16[1024,1024]{1,0:T(8,128)(2,1)}, f32[32,2048]{1,0:T(8,128)}) custom-call(bf16[1024,1024]{1,0:T(8,128)(2,1)S(1)} %get-tuple-element.4.posts, f32[32,2048]{1,0:T(8,128)S(1)} %get-tuple-element.5.refs), custom_call_target="tpu_custom_call" | custom-call | tf_op jit(solution)/shard_map/pallas_call | solution.py:558
